TPU v7x, 32 devices: a whole 2x2x4 slice. The times are simulated.
32 devices in a mesh: rep: 4 (over x, core), own: 8 (over z, y).
Axes of the slice: x: 2, y: 2, z: 4, core: 2. Of those that a mesh axis runs over, the one named last changes fastest.
Arguments:
- weights: float32 [4, 256, 8, 2048], P('rep', 'own'), may hold values from -6 to 6
- anchor: float32 [832, 8, 2048], P('own'), may hold values from -6 to 6
- momentum: float32 [832, 8, 2048], P('own'), may hold values from -3 to 3
- owner: int32 [256], replicated, may hold values from 0 to 7, as said below
- emb_weights: float32 [4, 1024, 2048], P('rep', 'own'), may hold values from -6 to 6
- emb_anchor: float32 [1024, 2048], P('own'), may hold values from -6 to 6
- emb_momentum: float32 [1024, 2048], P('own'), may hold values from -3 to 3
- sketch: float32 [64, 2048], replicated, may hold values from -0.125 to 0.125
- inv_root: float32 [64, 64], replicated
Outputs:
- new_weights: float32 [256, 8, 2048], P('own')
- new_momentum: float32 [832, 8, 2048], P('own')
- new_embedding: float32 [1024, 2048], P('own')
- new_emb_momentum: float32 [1024, 2048], P('own')
Inputs may be any that keep to these rules, and one draw needn't show every extreme that they name: Each owner holds at least 8 and at most 104 tiles, and some owner holds exactly 104. Of the 32 tiles of one aligned block, at most 13 have the same owner, and some block reaches 13.
All inputs are finite; a program needn't handle non-finite values.
Results may differ from a plain program's by a relative error of at most 0.0001.
Values sent between devices are 32-bit elements; how exact they have to be, the bound alone decides.
A program may use at most 128 MiB of HBM per device.

v0:
```python
import jax
import jax.numpy as jnp
from jax import lax
from jax.sharding import PartitionSpec as P

OUTER_RATE = 0.7
OUTER_MOMENTUM = 0.9


def owner_tables(owner, tiles_dev, per_pair, capacity, own_index, own_count):
    tile_count = owner.shape[0]
    tile_ids = jnp.arange(tile_count, dtype=jnp.int32)
    block_of = tile_ids // tiles_dev
    same_owner = owner[:, None] == owner[None, :]
    earlier = tile_ids[None, :] < tile_ids[:, None]
    slot_rank = jnp.sum(same_owner & earlier, axis=1, dtype=jnp.int32)
    pair_rank = jnp.sum(
        same_owner & earlier & (block_of[:, None] == block_of[None, :]), axis=1, dtype=jnp.int32
    )
    local_owner = lax.dynamic_slice_in_dim(owner, own_index * tiles_dev, tiles_dev)
    local_pair = lax.dynamic_slice_in_dim(pair_rank, own_index * tiles_dev, tiles_dev)
    dest_ids = jnp.arange(own_count, dtype=jnp.int32)[:, None, None]
    pair_ids = jnp.arange(per_pair, dtype=jnp.int32)[None, :, None]
    outgoing_match = (local_owner[None, None, :] == dest_ids) & (
        local_pair[None, None, :] == pair_ids
    )
    local_ids = jnp.arange(tiles_dev, dtype=jnp.int32)[None, None, :]
    local_pick = jnp.sum(jnp.where(outgoing_match, local_ids, 0), axis=2).reshape(-1)
    shard_read = local_owner * per_pair + local_pair
    held_here = owner == own_index
    slot_ids = jnp.arange(capacity, dtype=jnp.int32)[:, None]
    holder_match = held_here[None, :] & (slot_rank[None, :] == slot_ids)
    owner_read = jnp.sum(
        jnp.where(holder_match, (block_of * per_pair + pair_rank)[None, :], 0), axis=1
    )
    is_filled = jnp.any(holder_match, axis=1)
    return_match = (
        held_here[None, None, :]
        & (block_of[None, None, :] == dest_ids)
        & (pair_rank[None, None, :] == pair_ids)
    )
    owner_pick = jnp.sum(jnp.where(return_match, slot_rank[None, None, :], 0), axis=2).reshape(-1)
    return (local_pick, shard_read, owner_read, is_filled, owner_pick)


def local(
    weights, anchor, momentum, owner, emb_weights, emb_anchor, emb_momentum, sketch, inv_root
):
    own_count = lax.axis_size("own")
    rep_count = lax.axis_size("rep")
    own_index = lax.axis_index("own")
    tiles_dev = weights.shape[1]
    tile_rows = weights.shape[2]
    width = weights.shape[3]
    capacity = anchor.shape[0]
    half_tiles = min(tiles_dev // 2, own_count)
    hot_count = max(own_count // 4, 1)
    per_pair = (tiles_dev - half_tiles) // hot_count + 1
    local_pick, shard_read, owner_read, is_filled, owner_pick = owner_tables(
        owner, tiles_dev, per_pair, capacity, own_index, own_count
    )
    rep_index = lax.axis_index("rep")
    part = width // rep_count
    mean_part = lax.psum_scatter(weights[0], "rep", scatter_dimension=2, tiled=True) * (
        1.0 / rep_count
    )
    anchor_part = lax.dynamic_slice_in_dim(anchor, rep_index * part, part, axis=2)
    momentum_part = lax.dynamic_slice_in_dim(momentum, rep_index * part, part, axis=2)
    held_part = anchor_part - OUTER_RATE * (
        (1.0 + OUTER_MOMENTUM) * anchor_part + OUTER_MOMENTUM * OUTER_MOMENTUM * momentum_part
    )

    def exchange(tiles, pick):
        sent = jnp.take(tiles, pick, axis=0).reshape(own_count, per_pair, tile_rows, part)
        return lax.all_to_all(sent, "own", split_axis=0, concat_axis=0, tiled=True).reshape(
            own_count * per_pair, tile_rows, part
        )

    landed = jnp.take(exchange(held_part, owner_pick), shard_read, axis=0)
    new_part = landed + OUTER_RATE * (1.0 + OUTER_MOMENTUM) * mean_part
    placed_part = jnp.take(exchange(mean_part, local_pick), owner_read, axis=0)
    new_weights = lax.all_gather(new_part, "rep", axis=2, tiled=True)
    weight_mean = lax.all_gather(placed_part, "rep", axis=2, tiled=True)
    moved = OUTER_MOMENTUM * momentum + (anchor - weight_mean)
    new_momentum = jnp.where(is_filled[:, None, None], moved, 0.0)
    highest = lax.Precision.HIGHEST
    emb_diff = emb_anchor - emb_weights[0]
    local_sketch = lax.dot_general(
        sketch,
        emb_diff,
        (((1,), (1,)), ((), ())),
        precision=highest,
        preferred_element_type=jnp.float32,
    )
    sketch_mean = lax.psum(local_sketch, "rep") * (1.0 / rep_count)
    basis_rows = jnp.dot(
        inv_root, sketch_mean, precision=highest, preferred_element_type=jnp.float32
    )
    local_factor = jnp.dot(
        basis_rows, emb_diff, precision=highest, preferred_element_type=jnp.float32
    )
    factor = lax.psum(local_factor, ("rep", "own")) * (1.0 / rep_count)
    approx = lax.dot_general(
        basis_rows,
        factor,
        (((0,), (0,)), ((), ())),
        precision=highest,
        preferred_element_type=jnp.float32,
    )
    new_emb_momentum = OUTER_MOMENTUM * emb_momentum + approx
    new_embedding = emb_anchor - OUTER_RATE * (approx + OUTER_MOMENTUM * new_emb_momentum)
    return (new_weights, new_momentum, new_embedding, new_emb_momentum)


def solution(mesh):
    placed = (
        P("rep", "own", None, None),
        P("own", None, None),
        P("own", None, None),
        P(),
        P("rep", "own", None),
        P("own", None),
        P("own", None),
        P(),
        P(),
    )
    return jax.shard_map(
        local,
        mesh=mesh,
        in_specs=placed,
        out_specs=(P("own", None, None), P("own", None, None), P("own", None), P("own", None)),
        check_vma=False,
    )
```

profile of v0, /device:TPU:0, one launch (start us, length us, event | category | flops | bytes accessed | tf_op | source)
XLA Modules:
  0.0 231.5 jit_solution(14581863288011839253)
XLA Ops:
  8.0 0.0 copy-start
  8.0 0.0 copy-start.6
  8.0 0.0 reduce-scatter.2.cloned.1.call-start
  8.1 0.7 reduce-scatter.2.cloned.1.call-update
  8.8 0.0 copy-done.6
  8.8 0.3 convert_reduce_fusion.1
  9.1 0.3 select_reduce_fusion.1
  9.4 0.1 copy.13
  9.5 0.1 reshape.229
  9.6 3.6 %multiply_subtract_fusion = f32[104,8,512]{2,1,0:T(8,128)} fusion(f32[104,8,2048]{2,1,0:T(8,128)} %param.13, s32[]{:T(128)S(6)} %select_n.88, f32[104,8,2048]{2,1,0:T(8,128)} %param.12), kind=kLoop, calls=%fused_computation.5 | loop fusion | flops 2129920 | bytes 5111812 | tf_op jit(solution)/shard_map/sub | solution.py:69
  13.2 2.1 gather_fusion.2
  15.3 1.4 broadcast_select_fusion.1
  16.7 0.0 copy-start.1
  16.7 0.0 copy-start.2
  16.7 7.5 %all-to-all-start = ((f32[8,13,8,512]{3,2,1,0:T(8,128)}), f32[8,13,8,512]{3,2,1,0:T(8,128)}, u32[]{:S(2)}, u32[]{:S(2)}) async-start(f32[8,13,8,512]{3,2,1,0:T(8,128)} %bitcast), calls=%async_computation | async-start | bytes 3407872 | tf_op jit(solution)/shard_map/all_to_all | solution.py:75
  24.2 0.0 copy-start.5
  24.2 0.0 all-reduce.2.cloned.1.call-start
  24.3 0.0 copy-done
  24.3 0.0 copy-done.1
  24.3 0.0 copy-done.2
  24.3 1.2 convolution_bitcast_fusion
  25.5 11.7 %psum.14 = f32[64,128]{1,0:T(8,128)S(1)} all-reduce(f32[64,128]{1,0:T(8,128)S(1)} %convolution_bitcast_fusion), channel_id=1, replica_groups=mesh['rep'=4,'own'=8] {'rep'}, use_global_device_ids=true, to_apply=%region_7.9 | all-reduce | flops 8192 | bytes 65536 | tf_op jit(solution)/shard_map/psum | solution.py:95
  37.2 0.0 copy-done.5
  37.2 0.2 fusion.7
  37.3 1.5 fusion.2
  38.9 0.0 all-reduce.2.cloned.1.call-update
  38.9 0.1 compare_and_fusion.3
  39.0 0.3 select_reduce_fusion.2
  39.3 0.1 copy.15
  39.4 0.1 reshape.232
  39.5 0.1 copy.14
  39.6 25.8 %all-to-all-done = f32[8,13,8,512]{3,2,1,0:T(8,128)} async-done(((f32[8,13,8,512]{3,2,1,0:T(8,128)}), f32[8,13,8,512]{3,2,1,0:T(8,128)}, u32[]{:S(2)}, u32[]{:S(2)}) %all-to-all-start) | async-done | bytes 1703968 | tf_op jit(solution)/shard_map/all_to_all | solution.py:75
  65.5 2.0 gather_fusion
  67.5 0.0 reduce-scatter.2.cloned.1.call-done
  67.5 2.0 broadcast_multiply_fusion
  69.5 1.9 gather_fusion.1
  71.5 2.8 %broadcast_select_fusion.2 = f32[8,13,8,512]{3,2,1,0:T(8,128)} fusion(f32[8,13,8,512]{3,2,1,0:T(8,128)} %bitcast.17, pred[8,13]{1,0:T(8,128)(4,1)S(1)} %copy.14), kind=kLoop, calls=%fused_computation.12 | loop fusion | flops 425984 | bytes 3407976 | tf_op jit(solution)/shard_map/jit(_take)/select_n | solution.py:74
  74.3 3.7 %all-to-all-start.1 = ((f32[8,13,8,512]{3,2,1,0:T(8,128)}), f32[8,13,8,512]{3,2,1,0:T(8,128)S(1)}, u32[]{:S(2)}, u32[]{:S(2)}) async-start(f32[8,13,8,512]{3,2,1,0:T(8,128)} %broadcast_select_fusion.2), calls=%async_computation.2 | async-start | bytes 3407872 | tf_op jit(solution)/shard_map/all_to_all | solution.py:75
  78.0 0.0 all-gather.3.cloned.1.call-start
  78.0 0.7 all-gather.3.cloned.1.call-update
  78.7 0.0 all-gather.5.cloned.1.call-start
  78.8 0.1 select_reduce_fusion
  78.9 39.9 %all-to-all-done.1 = f32[8,13,8,512]{3,2,1,0:T(8,128)S(1)} async-done(((f32[8,13,8,512]{3,2,1,0:T(8,128)}), f32[8,13,8,512]{3,2,1,0:T(8,128)S(1)}, u32[]{:S(2)}, u32[]{:S(2)}) %all-to-all-start.1) | async-done | bytes 1703968 | tf_op jit(solution)/shard_map/all_to_all | solution.py:75
  118.9 1.9 gather_fusion.3
  120.8 2.8 %broadcast_select_fusion = f32[104,8,512]{2,1,0:T(8,128)} fusion(f32[104,8,512]{2,1,0:T(8,128)} %gather_fusion.3, pred[104]{0:T(512)(128)(4,1)S(1)} %compare_and_fusion.1), kind=kLoop, calls=%fused_computation.10 | loop fusion | flops 425984 | bytes 3407976 | tf_op jit(solution)/shard_map/jit(_take)/select_n | solution.py:81
  123.6 0.0 copy-start.4
  123.6 0.0 all-gather.5.cloned.1.call-update
  123.7 0.1 fusion.6
  123.8 84.6 %all-reduce.2.cloned.1.call-done = f32[64,2048]{1,0:T(8,128)} async-done(((f32[64,2048]{1,0:T(8,128)}), f32[64,2048]{1,0:T(8,128)}) %all-reduce.2.cloned.1.call-update) | async-done | bytes 524304 | tf_op jit(solution)/shard_map/psum | solution.py:102
  208.4 0.0 copy-done.4
  208.4 3.6 %multiply_subtract_fusion.1 = (f32[128,2048]{1,0:T(8,128)}, f32[128,2048]{1,0:T(8,128)}) fusion(f32[128,2048]{1,0:T(8,128)S(1)} %copy-done.1, f32[128,2048]{1,0:T(8,128)S(1)} %copy-done.4, f32[128,64]{0,1:T(8,128)S(1)} %fusion.7, f32[64,2048]{1,0:T(8,128)} %all-reduce.2.cloned.1.call-done), kind=kOutput, calls=%fused_computation.8 | convolution fusion | flops 203030528 | bytes 4751360 | tf_op jit(solution)/shard_map/dot_general | solution.py:103
  212.0 0.0 all-gather.3.cloned.1.call-done
  212.0 0.0 all-gather.5.cloned.1.call-done
  212.0 0.0 copy-start.3
  212.0 11.0 %add_select_fusion = f32[104,8,2048]{2,1,0:T(8,128)} fusion(f32[104,8,2048]{2,1,0:T(8,128)} %param.12, f32[104,8,2048]{2,1,0:T(8,128)} %all-gather.5.cloned.1.call-done, f32[104,8,2048]{2,1,0:T(8,128)} %param.13, pred[104]{0:T(512)(128)(4,1)S(1)} %fusion.6), kind=kLoop, calls=%fused_computation.4 | loop fusion | flops 6815744 | bytes 27263080 | tf_op jit(solution)/shard_map/jit(_where)/select_n | solution.py:85
  223.0 0.0 copy-done.3
  223.0 1.3 copy.18
  (17 shorter events, 0.1 us)
Async XLA Ops:
  8.0 16.3 %copy-start = (f32[64,2048]{1,0:T(8,128)S(1)}, f32[64,2048]{1,0:T(8,128)}, u32[]{:S(2)}) copy-start(f32[64,2048]{1,0:T(8,128)} %param.18) | copy-start | bytes 1572868
  8.0 0.8 copy-start.6
  8.0 59.5 %reduce-scatter.2.cloned.1.call-start = ((), (), s32[]{:S(2)}) async-start(), calls=%async_computation.3 | async-start | bytes 2621440 | tf_op jit(solution)/shard_map/reduce_scatter | solution.py:64
  16.7 7.6 %copy-start.1 = (f32[128,2048]{1,0:T(8,128)S(1)}, f32[128,2048]{1,0:T(8,128)}, u32[]{:S(2)}) copy-start(f32[128,2048]{1,0:T(8,128)} %param.16) | copy-start | bytes 3145732
  16.7 7.6 %copy-start.2 = (f32[1,128,2048]{2,1,0:T(8,128)S(1)}, f32[1,128,2048]{2,1,0:T(8,128)}, u32[]{:S(2)}) copy-start(f32[1,128,2048]{2,1,0:T(8,128)} %param.15) | copy-start | bytes 3145732
  16.7 48.8 %all-to-all-start = ((f32[8,13,8,512]{3,2,1,0:T(8,128)}), f32[8,13,8,512]{3,2,1,0:T(8,128)}, u32[]{:S(2)}, u32[]{:S(2)}) async-start(f32[8,13,8,512]{3,2,1,0:T(8,128)} %bitcast), calls=%async_computation | async-start | bytes 3407872 | tf_op jit(solution)/shard_map/all_to_all | solution.py:75
  24.2 12.9 %copy-start.5 = (f32[64,64]{1,0:T(8,128)S(1)}, f32[64,64]{1,0:T(8,128)}, u32[]{:S(2)}) copy-start(f32[64,64]{1,0:T(8,128)} %param.19) | copy-start | bytes 49156
  24.2 184.2 %all-reduce.2.cloned.1.call-start = ((), (), s32[]{:S(2)}) async-start(), calls=%async_computation.6 | async-start | bytes 1048576 | tf_op jit(solution)/shard_map/psum | solution.py:102
  74.3 44.6 %all-to-all-start.1 = ((f32[8,13,8,512]{3,2,1,0:T(8,128)}), f32[8,13,8,512]{3,2,1,0:T(8,128)S(1)}, u32[]{:S(2)}, u32[]{:S(2)}) async-start(f32[8,13,8,512]{3,2,1,0:T(8,128)} %broadcast_select_fusion.2), calls=%async_computation.2 | async-start | bytes 3407872 | tf_op jit(solution)/shard_map/all_to_all | solution.py:75
  78.0 134.0 %all-gather.3.cloned.1.call-start = ((), (), s32[]{:S(2)}) async-start(), calls=%async_computation.4 | async-start | bytes 2621440 | tf_op jit(solution)/shard_map/all_gather | solution.py:82
  78.7 133.3 %all-gather.5.cloned.1.call-start = ((), (), s32[]{:S(2)}) async-start(), calls=%async_computation.5 | async-start | bytes 8519680 | tf_op jit(solution)/shard_map/all_gather | solution.py:83
  123.6 84.8 %copy-start.4 = (f32[128,2048]{1,0:T(8,128)S(1)}, f32[128,2048]{1,0:T(8,128)}, u32[]{:S(2)}) copy-start(f32[128,2048]{1,0:T(8,128)} %param.17) | copy-start | bytes 3145732
  212.0 11.0 %copy-start.3 = (f32[32,8,2048]{2,1,0:T(8,128)S(1)}, f32[32,8,2048]{2,1,0:T(8,128)}, u32[]{:S(2)}) copy-start(f32[32,8,2048]{2,1,0:T(8,128)} %all-gather.3.cloned.1.call-done) | copy-start | bytes 6291460
Sparse Core Ops, SparseCore 0:
  11.4 34.3 reduce-scatter.1
  81.0 23.9 all-gather.2
  123.8 48.6 all-gather.4
Sparse Core Ops, SparseCore 1:
  39.0 169.4 all-reduce.1
where the time goes:
time: 232 us; the launch traced here: 231 us
  waiting for transfers between devices  152 us (66%)
  other arithmetic  25 us (11%)
  between operations  15.4 us (7%)
  blocking collectives  11.7 us (5%)
  starting transfers between devices  11.4 us (5%)
  local copies, waits for them, and re-layouts  9.77 us (4%)
  matrix products  6.43 us (3%)
    psum x1, waiting for transfers between devices, local(): factor = lax.psum(local_factor, ('rep', 'own')) * (1.0 / rep_count)  84.6 us
    all_to_all x2, waiting for transfers between devices, exchange(): lax.all_to_all(sent, 'own', split_axis=0, concat_axis=0, tiled=True)  65.8 us
    psum x1, blocking collectives, local(): sketch_mean = lax.psum(local_sketch, 'rep') * (1.0 / rep_count)  11.7 us
    all_to_all x2, starting transfers between devices, exchange(): lax.all_to_all(sent, 'own', split_axis=0, concat_axis=0, tiled=True)  11.2 us
    select_n x1, other arithmetic, local(): new_momentum = jnp.where(is_filled[:, None, None], moved, 0.0)  11 us
  transfers between devices with their start and end apart: 6, of which 3 were waited for; matrix products, arithmetic and copies ran while one was open for 12% of the time, Pallas kernels for 0%

commit v1 on v0

--- a/solution.py
+++ b/solution.py
@@ -99,7 +99,7 @@
     local_factor = jnp.dot(
         basis_rows, emb_diff, precision=highest, preferred_element_type=jnp.float32
     )
-    factor = lax.psum(local_factor, ("rep", "own")) * (1.0 / rep_count)
+    factor = lax.psum(lax.psum(local_factor, "own"), "rep") * (1.0 / rep_count)
     approx = lax.dot_general(
         basis_rows,
         factor,

time: 232 us -> 249 us (1.073)
  waiting for transfers between devices: 152 us -> 166 us
    all_gather x1, waiting for transfers between devices: 0.01 us -> 48 us  [local(): weight_mean = lax.all_gather(placed_part, 'rep', axis=2, tiled=True)]
    all_to_all x2, waiting for transfers between devices: 65.8 us -> 37.9 us  [exchange(): lax.all_to_all(sent, 'own', split_axis=0, concat_axis=0, tiled=True)]
    psum x1 -> x2, waiting for transfers between devices: 84.6 us -> 78.6 us  [local(): factor = lax.psum(lax.psum(local_factor, 'own'), 'rep') * (1.0 / rep_count)]
  transfers between devices with their start and end apart: 6 -> 7, of which waited for: 3 -> 3; matrix products, arithmetic and copies ran while one was open for 12% -> 10% of each run, Pallas kernels for 0% -> 0%
where the time goes in v1:
time: 249 us
  waiting for transfers between devices  166 us (67%)
  other arithmetic  25.1 us (10%)
  between operations  15.9 us (6%)
  blocking collectives  12.9 us (5%)
  local copies, waits for them, and re-layouts  11.3 us (5%)
  starting transfers between devices  9.95 us (4%)
  matrix products  7.97 us (3%)
    psum x2, waiting for transfers between devices, local(): factor = lax.psum(lax.psum(local_factor, 'own'), 'rep') * (1.0 / rep_count)  78.6 us
    all_gather x1, waiting for transfers between devices, local(): weight_mean = lax.all_gather(placed_part, 'rep', axis=2, tiled=True)  48 us
    all_to_all x2, waiting for transfers between devices, exchange(): lax.all_to_all(sent, 'own', split_axis=0, concat_axis=0, tiled=True)  37.9 us
    psum x1, blocking collectives, local(): sketch_mean = lax.psum(local_sketch, 'rep') * (1.0 / rep_count)  12.9 us
    select_n x1, other arithmetic, local(): new_momentum = jnp.where(is_filled[:, None, None], moved, 0.0)  11 us
    all_to_all x2, starting transfers between devices, exchange(): lax.all_to_all(sent, 'own', split_axis=0, concat_axis=0, tiled=True)  9.75 us
  transfers between devices with their start and end apart: 7, of which 3 were waited for; matrix products, arithmetic and copies ran while one was open for 10% of the time, Pallas kernels for 0%

profile of v1, /device:TPU:0, one launch (start us, length us, event | category | flops | bytes accessed | tf_op | source)
XLA Modules:
  0.0 248.6 jit_solution(1214205254335328672)
XLA Ops:
  8.0 0.0 copy-start
  8.0 0.0 copy-start.2
  8.0 0.0 copy-start.1
  8.0 0.0 copy-start.5
  8.0 0.0 all-reduce.3.cloned.1.call-start
  8.1 1.0 copy-done
  9.0 2.7 %convolution_bitcast_fusion = f32[64,128]{1,0:T(8,128)S(1)} fusion(f32[64,2048]{1,0:T(8,128)S(1)} %copy-done, f32[128,2048]{1,0:T(8,128)} %param.16, f32[1,128,2048]{2,1,0:T(8,128)} %param.15), kind=kOutput, calls=%fused_computation.6 | convolution fusion | flops 201588736 | bytes 2654208 | tf_op jit(solution)/shard_map/dot_general | solution.py:88
  11.8 12.9 %psum.21 = f32[64,128]{1,0:T(8,128)S(1)} all-reduce(f32[64,128]{1,0:T(8,128)S(1)} %convolution_bitcast_fusion), channel_id=1, replica_groups=mesh['rep'=4,'own'=8] {'rep'}, use_global_device_ids=true, to_apply=%region_7.9 | all-reduce | flops 8192 | bytes 65536 | tf_op jit(solution)/shard_map/psum | solution.py:95
  24.6 0.0 copy-done.5
  24.6 0.2 fusion.7
  24.8 0.0 copy-done.2
  24.8 0.0 copy-done.1
  24.8 1.5 fusion.2
  26.4 0.0 copy-start.6
  26.4 0.0 all-reduce.3.cloned.1.call-update
  26.4 0.0 reduce-scatter.2.cloned.1.call-start
  26.4 0.5 reduce-scatter.2.cloned.1.call-update
  27.0 0.1 copy-done.6
  27.0 0.3 convert_reduce_fusion.1
  27.3 0.3 select_reduce_fusion.1
  27.6 0.1 copy.13
  27.7 0.1 reshape.229
  27.8 3.6 %multiply_subtract_fusion = f32[104,8,512]{2,1,0:T(8,128)} fusion(f32[104,8,2048]{2,1,0:T(8,128)} %param.13, s32[]{:T(128)S(6)} %select_n.88, f32[104,8,2048]{2,1,0:T(8,128)} %param.12), kind=kLoop, calls=%fused_computation.5 | loop fusion | flops 2129920 | bytes 5111812 | tf_op jit(solution)/shard_map/sub | solution.py:69
  31.4 2.2 gather_fusion.2
  33.6 1.4 broadcast_select_fusion.1
  35.0 5.8 %all-to-all-start = ((f32[8,13,8,512]{3,2,1,0:T(8,128)}), f32[8,13,8,512]{3,2,1,0:T(8,128)S(1)}, u32[]{:S(2)}, u32[]{:S(2)}) async-start(f32[8,13,8,512]{3,2,1,0:T(8,128)} %bitcast), calls=%async_computation | async-start | bytes 3407872 | tf_op jit(solution)/shard_map/all_to_all | solution.py:75
  40.9 0.0 all-reduce.5.cloned.1.call-start
  40.9 0.1 compare_and_fusion.3
  41.0 0.3 select_reduce_fusion.2
  41.3 0.1 copy.15
  41.4 0.1 reshape.232
  41.5 0.1 copy.14
  41.6 78.6 %all-reduce.3.cloned.1.call-done = f32[64,2048]{1,0:T(8,128)} async-done(((f32[64,2048]{1,0:T(8,128)}), f32[64,2048]{1,0:T(8,128)}) %all-reduce.3.cloned.1.call-update) | async-done | bytes 524304 | tf_op jit(solution)/shard_map/psum | solution.py:102
  120.2 0.0 all-reduce.5.cloned.1.call-update
  120.3 0.0 all-to-all-done
  120.3 1.4 gather_fusion
  121.6 0.0 reduce-scatter.2.cloned.1.call-done
  121.6 2.1 broadcast_multiply_fusion
  123.8 1.9 gather_fusion.1
  125.7 2.8 %broadcast_select_fusion.2 = f32[8,13,8,512]{3,2,1,0:T(8,128)} fusion(f32[8,13,8,512]{3,2,1,0:T(8,128)} %bitcast.17, pred[8,13]{1,0:T(8,128)(4,1)S(1)} %copy.14), kind=kLoop, calls=%fused_computation.12 | loop fusion | flops 425984 | bytes 3407976 | tf_op jit(solution)/shard_map/jit(_take)/select_n | solution.py:74
  128.5 3.9 %all-to-all-start.1 = ((f32[8,13,8,512]{3,2,1,0:T(8,128)}), f32[8,13,8,512]{3,2,1,0:T(8,128)S(1)}, u32[]{:S(2)}, u32[]{:S(2)}) async-start(f32[8,13,8,512]{3,2,1,0:T(8,128)} %broadcast_select_fusion.2), calls=%async_computation.2 | async-start | bytes 3407872 | tf_op jit(solution)/shard_map/all_to_all | solution.py:75
  132.4 0.0 all-gather.3.cloned.1.call-start
  132.5 0.5 all-gather.3.cloned.1.call-update
  133.0 0.0 all-gather.5.cloned.1.call-start
  133.1 0.1 select_reduce_fusion
  133.2 37.9 %all-to-all-done.1 = f32[8,13,8,512]{3,2,1,0:T(8,128)S(1)} async-done(((f32[8,13,8,512]{3,2,1,0:T(8,128)}), f32[8,13,8,512]{3,2,1,0:T(8,128)S(1)}, u32[]{:S(2)}, u32[]{:S(2)}) %all-to-all-start.1) | async-done | bytes 1703968 | tf_op jit(solution)/shard_map/all_to_all | solution.py:75
  171.1 1.9 gather_fusion.3
  173.0 2.8 %broadcast_select_fusion = f32[104,8,512]{2,1,0:T(8,128)} fusion(f32[104,8,512]{2,1,0:T(8,128)} %gather_fusion.3, pred[104]{0:T(512)(128)(4,1)S(1)} %compare_and_fusion.1), kind=kLoop, calls=%fused_computation.10 | loop fusion | flops 425984 | bytes 3407976 | tf_op jit(solution)/shard_map/jit(_take)/select_n | solution.py:81
  175.8 0.0 copy-start.4
  175.8 0.0 all-gather.5.cloned.1.call-update
  175.9 0.1 fusion.6
  176.0 0.0 all-reduce.5.cloned.1.call-done
  176.0 1.1 copy-done.4
  177.1 3.6 %multiply_subtract_fusion.1 = (f32[128,2048]{1,0:T(8,128)}, f32[128,2048]{1,0:T(8,128)}) fusion(f32[128,2048]{1,0:T(8,128)S(1)} %copy-done.1, f32[128,2048]{1,0:T(8,128)S(1)} %copy-done.4, f32[128,64]{0,1:T(8,128)S(1)} %fusion.7, f32[64,2048]{1,0:T(8,128)} %all-reduce.5.cloned.1.call-done), kind=kOutput, calls=%fused_computation.8 | convolution fusion | flops 203030528 | bytes 4751360 | tf_op jit(solution)/shard_map/dot_general | solution.py:103
  180.6 0.0 all-gather.3.cloned.1.call-done
  180.6 48.0 %all-gather.5.cloned.1.call-done = f32[104,8,2048]{2,1,0:T(8,128)} async-done(((f32[104,8,512]{2,1,0:T(8,128)}), f32[104,8,2048]{2,1,0:T(8,128)}) %all-gather.5.cloned.1.call-update) | async-done | bytes 6815760 | tf_op jit(solution)/shard_map/all_gather | solution.py:83
  228.6 0.0 copy-start.3
  228.6 11.0 %add_select_fusion = f32[104,8,2048]{2,1,0:T(8,128)} fusion(f32[104,8,2048]{2,1,0:T(8,128)} %param.12, f32[104,8,2048]{2,1,0:T(8,128)} %all-gather.5.cloned.1.call-done, f32[104,8,2048]{2,1,0:T(8,128)} %param.13, pred[104]{0:T(512)(128)(4,1)S(1)} %fusion.6), kind=kLoop, calls=%fused_computation.4 | loop fusion | flops 6815744 | bytes 27263080 | tf_op jit(solution)/shard_map/jit(_where)/select_n | solution.py:85
  239.7 0.0 copy-done.3
  239.7 1.3 copy.19
  (17 shorter events, 0.1 us)
Async XLA Ops:
  8.0 1.0 copy-start
  8.0 16.8 %copy-start.2 = (f32[1,128,2048]{2,1,0:T(8,128)S(1)}, f32[1,128,2048]{2,1,0:T(8,128)}, u32[]{:S(2)}) copy-start(f32[1,128,2048]{2,1,0:T(8,128)} %param.15) | copy-start | bytes 3145732
  8.0 16.8 %copy-start.1 = (f32[128,2048]{1,0:T(8,128)S(1)}, f32[128,2048]{1,0:T(8,128)}, u32[]{:S(2)}) copy-start(f32[128,2048]{1,0:T(8,128)} %param.16) | copy-start | bytes 3145732
  8.0 16.6 %copy-start.5 = (f32[64,64]{1,0:T(8,128)S(1)}, f32[64,64]{1,0:T(8,128)}, u32[]{:S(2)}) copy-start(f32[64,64]{1,0:T(8,128)} %param.19) | copy-start | bytes 49156
  8.0 112.2 %all-reduce.3.cloned.1.call-start = ((), (), s32[]{:S(2)}) async-start(), calls=%async_computation.6 | async-start | bytes 1048576 | tf_op jit(solution)/shard_map/psum | solution.py:102
  26.4 0.7 copy-start.6
  26.4 95.3 %reduce-scatter.2.cloned.1.call-start = ((), (), s32[]{:S(2)}) async-start(), calls=%async_computation.3 | async-start | bytes 2621440 | tf_op jit(solution)/shard_map/reduce_scatter | solution.py:64
  35.0 85.2 %all-to-all-start = ((f32[8,13,8,512]{3,2,1,0:T(8,128)}), f32[8,13,8,512]{3,2,1,0:T(8,128)S(1)}, u32[]{:S(2)}, u32[]{:S(2)}) async-start(f32[8,13,8,512]{3,2,1,0:T(8,128)} %bitcast), calls=%async_computation | async-start | bytes 3407872 | tf_op jit(solution)/shard_map/all_to_all | solution.py:75
  40.9 135.1 %all-reduce.5.cloned.1.call-start = ((), (), s32[]{:S(2)}) async-start(), calls=%async_computation.7 | async-start | bytes 1048576 | tf_op jit(solution)/shard_map/psum | solution.py:102
  128.5 42.6 %all-to-all-start.1 = ((f32[8,13,8,512]{3,2,1,0:T(8,128)}), f32[8,13,8,512]{3,2,1,0:T(8,128)S(1)}, u32[]{:S(2)}, u32[]{:S(2)}) async-start(f32[8,13,8,512]{3,2,1,0:T(8,128)} %broadcast_select_fusion.2), calls=%async_computation.2 | async-start | bytes 3407872 | tf_op jit(solution)/shard_map/all_to_all | solution.py:75
  132.4 48.2 %all-gather.3.cloned.1.call-start = ((), (), s32[]{:S(2)}) async-start(), calls=%async_computation.4 | async-start | bytes 2621440 | tf_op jit(solution)/shard_map/all_gather | solution.py:82
  133.0 95.6 %all-gather.5.cloned.1.call-start = ((), (), s32[]{:S(2)}) async-start(), calls=%async_computation.5 | async-start | bytes 8519680 | tf_op jit(solution)/shard_map/all_gather | solution.py:83
  175.8 1.2 copy-start.4
  228.6 11.0 %copy-start.3 = (f32[32,8,2048]{2,1,0:T(8,128)S(1)}, f32[32,8,2048]{2,1,0:T(8,128)}, u32[]{:S(2)}) copy-start(f32[32,8,2048]{2,1,0:T(8,128)} %all-gather.3.cloned.1.call-done) | copy-start | bytes 6291460
Sparse Core Ops, SparseCore 0:
  26.5 93.6 all-reduce.2
Sparse Core Ops, SparseCore 1:
  29.4 31.6 reduce-scatter.1
  120.3 32.4 all-reduce.4
  154.8 22.4 all-gather.2
  179.4 49.2 all-gather.4
